TPU v7x, 32 devices: a whole 2x2x4 slice. The times are simulated.
32 devices in a mesh: parts: 1, axial: 8 (over y, x, core), radial: 4 (over z).
Axes of the slice: x: 2, y: 2, z: 4, core: 2. Of those that a mesh axis runs over, the one named last changes fastest.
Arguments:
- inputs: bfloat16 [64, 64, 8192], P(None, 'radial', ('parts', 'axial')), may hold values from -6 to 6
- saved_pre: bfloat16 [64, 64, 8192], P(None, 'radial', ('parts', 'axial')), may hold values from -6 to 6
- cotangent: bfloat16 [64, 64, 8192], P(None, 'radial', ('parts', 'axial')), may hold values from -24 to 24
- pointwise_weight: bfloat16 [64, 64], replicated, may hold values from -0.75 to 0.75
- spectral_weight: bfloat16 [32, 256, 64, 128], P('radial', 'axial'), may hold values from -3 to 3
Outputs:
- input_grad: bfloat16 [64, 64, 8192], P(None, 'radial', ('parts', 'axial'))
- spectral_grad: float32 [32, 256, 64, 128], P('radial', ('parts', 'axial'))
- weight_grad: float32 [64, 64], P('parts')
All inputs are finite; a program needn't handle non-finite values.
Results may differ from a plain program's by a relative error of at most 0.0053.
Values may be sent and summed in bfloat16 or wider, within the bound.
No kernel may reach another device: no remote copies, remote signals or barrier semaphores. Data moves between devices by JAX's collectives and lax.ppermute only.
A program may use at most 128 MiB of HBM per device.

v0:
```python
import math
import jax
import jax.numpy as jnp
from jax import lax
from jax.sharding import PartitionSpec as P

KA = 256
KR = 32


def axial_table(first, count, modes, total):
    points = first + jnp.arange(count, dtype=jnp.int32)
    orders = jnp.arange(modes, dtype=jnp.int32)
    phase = (points[:, None] * orders[None, :] % total).astype(jnp.float32) * (
        2.0 * math.pi / total
    )
    return (
        jnp.stack([jnp.cos(phase), -jnp.sin(phase)], axis=2)
        .reshape(count, 2 * modes)
        .astype(jnp.bfloat16)
    )


def radial_table(count, rows_first, rows_count, kept, total):
    orders = jnp.arange(count, dtype=jnp.int32)
    freqs = orders + jnp.where(orders >= kept // 2, total - kept, 0).astype(jnp.int32)
    rows = rows_first + jnp.arange(rows_count, dtype=jnp.int32)
    phase = (freqs[:, None] * rows[None, :] % total).astype(jnp.float32) * (2.0 * math.pi / total)
    return (jnp.cos(phase), jnp.sin(phase))


def gelu_slope(pre):
    value = pre.astype(jnp.float32)
    return 0.5 * (1.0 + jax.scipy.special.erf(value / math.sqrt(2.0))) + value * jnp.exp(
        -0.5 * value * value
    ) / math.sqrt(2.0 * math.pi)


def to_modes(axial_part, cos_r, sin_r, own_ax, channels, rad_rows):
    split = axial_part.reshape(own_ax, 2, channels, rad_rows)
    real_in = split[:, 0]
    imag_in = split[:, 1]
    high = lax.Precision.HIGHEST
    real_out = jnp.einsum("qr,kcr->qkc", cos_r, real_in, precision=high) + jnp.einsum(
        "qr,kcr->qkc", sin_r, imag_in, precision=high
    )
    imag_out = jnp.einsum("qr,kcr->qkc", cos_r, imag_in, precision=high) - jnp.einsum(
        "qr,kcr->qkc", sin_r, real_in, precision=high
    )
    return (real_out, imag_out)


def body(inputs, saved_pre, cotangent, pointwise_weight, spectral_weight):
    high = lax.Precision.HIGHEST
    channels, rad_rows, ax_cols = inputs.shape
    n_axial = lax.axis_size("axial")
    n_radial = lax.axis_size("radial")
    ax_index = lax.axis_index("axial")
    rad_index = lax.axis_index("radial")
    axial_total = ax_cols * n_axial
    radial_total = rad_rows * n_radial
    own_ax = KA // n_axial
    grad_pre = (cotangent.astype(jnp.float32) * gelu_slope(saved_pre)).astype(jnp.bfloat16)
    table = axial_table(ax_index * ax_cols, ax_cols, KA, axial_total)
    columns = table
    part_in = jnp.einsum("cra,aj->jcr", inputs, columns, preferred_element_type=jnp.float32)
    part_grad = jnp.einsum("cra,aj->jcr", grad_pre, columns, preferred_element_type=jnp.float32)
    summed = lax.psum_scatter(
        jnp.concatenate(
            [
                part_in.reshape(2 * own_ax * lax.axis_size("axial"), -1),
                part_grad.reshape(2 * own_ax * lax.axis_size("axial"), -1),
            ],
            axis=1,
        ),
        "axial",
        scatter_dimension=0,
        tiled=True,
    )
    half = channels * rad_rows
    spec_in = summed[:, :half].reshape(2 * own_ax, channels, rad_rows)
    spec_grad = summed[:, half:].reshape(2 * own_ax, channels, rad_rows)
    cos_r, sin_r = radial_table(KR, rad_index * rad_rows, rad_rows, KR, radial_total)
    x_real, x_imag = to_modes(spec_in, cos_r, sin_r, own_ax, channels, rad_rows)
    g_real, g_imag = to_modes(spec_grad, cos_r, sin_r, own_ax, channels, rad_rows)
    stacked = jnp.stack([x_real, x_imag, g_real, g_imag], axis=1)
    owned = lax.psum_scatter(stacked, "radial", scatter_dimension=0, tiled=True)
    orders = ax_index * own_ax + jnp.arange(own_ax, dtype=jnp.int32)
    scales = jnp.where(orders == 0, 1.0, 2.0).astype(jnp.float32) / (radial_total * axial_total)
    x_real = owned[:, 0]
    x_imag = owned[:, 1]
    dy_real = owned[:, 2] * scales[None, :, None]
    dy_imag = owned[:, 3] * scales[None, :, None]
    grad_real = (
        x_real[..., :, None] * dy_real[..., None, :] + x_imag[..., :, None] * dy_imag[..., None, :]
    )
    grad_imag = (
        x_real[..., :, None] * dy_imag[..., None, :] - x_imag[..., :, None] * dy_real[..., None, :]
    )
    spectral_grad = jnp.concatenate([grad_real, grad_imag], axis=3)
    w_real = spectral_weight[..., :channels].astype(jnp.float32)
    w_imag = spectral_weight[..., channels:].astype(jnp.float32)
    dx_real = jnp.einsum("qkio,qko->qki", w_real, dy_real, precision=high) + jnp.einsum(
        "qkio,qko->qki", w_imag, dy_imag, precision=high
    )
    dx_imag = jnp.einsum("qkio,qko->qki", w_real, dy_imag, precision=high) - jnp.einsum(
        "qkio,qko->qki", w_imag, dy_real, precision=high
    )
    mode_grad = jnp.stack([dx_real, dx_imag], axis=1)
    row_first = rad_index * rad_rows
    piece = lax.all_gather(mode_grad, "radial", axis=0, tiled=True)
    cos_q, sin_q = radial_table(piece.shape[0], row_first, rad_rows, KR, radial_total)
    piece_real = piece[:, 0]
    piece_imag = piece[:, 1]
    out_real = jnp.einsum("qr,qkc->kcr", cos_q, piece_real, precision=high) - jnp.einsum(
        "qr,qkc->kcr", sin_q, piece_imag, precision=high
    )
    out_imag = jnp.einsum("qr,qkc->kcr", sin_q, piece_real, precision=high) + jnp.einsum(
        "qr,qkc->kcr", cos_q, piece_imag, precision=high
    )
    back = jnp.stack([out_real, out_imag], axis=1)
    lines_back = back.astype(jnp.bfloat16).reshape(2 * own_ax, channels * rad_rows)
    columns = table
    spectral_part = jnp.einsum(
        "jm,aj->ma",
        lax.all_gather(lines_back, "axial", axis=0, tiled=True),
        columns,
        preferred_element_type=jnp.float32,
    )
    flat_grad = grad_pre.reshape(channels, rad_rows * ax_cols)
    flat_in = inputs.reshape(channels, rad_rows * ax_cols)
    point_part = jnp.dot(pointwise_weight, flat_grad, preferred_element_type=jnp.float32)
    input_grad = (
        (point_part + spectral_part.reshape(channels, rad_rows * ax_cols))
        .astype(jnp.bfloat16)
        .reshape(channels, rad_rows, ax_cols)
    )
    local_weight = lax.dot_general(
        flat_in, flat_grad, (((1,), (1,)), ((), ())), preferred_element_type=jnp.float32
    )
    weight_grad = lax.psum(local_weight, ("axial", "radial")) / math.sqrt(
        radial_total * axial_total
    )
    return (input_grad, spectral_grad, weight_grad)


def solution(mesh):
    placed = (
        P(None, "radial", ("parts", "axial")),
        P(None, "radial", ("parts", "axial")),
        P(None, "radial", ("parts", "axial")),
        P(),
        P("radial", "axial", None, None),
    )
    return jax.shard_map(
        body,
        mesh=mesh,
        in_specs=placed,
        out_specs=(
            P(None, "radial", ("parts", "axial")),
            P("radial", ("parts", "axial"), None, None),
            P("parts", None),
        ),
        check_vma=False,
    )
```

profile of v0, /device:TPU:0, one launch (start us, length us, event | category | flops | bytes accessed | tf_op | source)
XLA Modules:
  0.0 311.8 jit_solution(6213764440670143054)
XLA Ops:
  7.2 5.0 %fusion.44 = (bf16[1024,256,1]{1,0,2:T(8,128)(2,1)S(1)}, bf16[1024,256,1]{1,0,2:T(8,128)(2,1)S(1)}) fusion(s32[1024]{0:T(1024)S(1)} %iota_add_fusion), kind=kLoop, calls=%fused_computation.67 | loop fusion | flops 4456448 | bytes 1052672 | tf_op jit(solution)/shard_map/cos | solution.py:18
  12.4 2.1 copy.31
  16.0 3.9 %fusion.9 = bf16[64,16,1024]{2,1,0:T(8,128)(2,1)S(1)} fusion(bf16[64,16,1024]{2,1,0:T(8,128)(2,1)} %param.6, bf16[64,16,1024]{2,1,0:T(8,128)(2,1)} %param.7), kind=kLoop, calls=%fused_computation.18 | loop fusion | flops 12582912 | bytes 6291456 | tf_op jit(solution)/shard_map/convert_element_type | solution.py:63
  22.5 2.5 pad_maximum_fusion.1
  25.7 53.6 %reduce-scatter.3.cloned.1.call-done = f32[64,2048]{1,0:T(8,128)} async-done(((f32[512,2048]{1,0:T(8,128)}), f32[64,2048]{1,0:T(8,128)}) %reduce-scatter.3.cloned.1.call-update) | async-done | bytes 524304 | tf_op jit(solution)/shard_map/reduce_scatter | solution.py:68
  80.3 2.0 reshape_reshape.6
  82.4 4.3 %fusion.41 = f32[32,32,64]{2,0,1:T(8,128)S(1)} fusion(f32[32,2,64,16]{3,2,1,0:T(8,128)} %reshape_reshape.6, s32[16]{0:T(128)S(1)} %iota_add_fusion.1, s32[32]{0:T(128)S(1)} %fusion.84), kind=kOutput, calls=%fused_computation.62 | convolution fusion | flops 12590080 | bytes 1310912 | tf_op jit(solution)/shard_map/qr,kcr->qkc/dot_general | solution.py:47
  86.7 4.3 %fusion.40 = f32[32,32,64]{2,0,1:T(8,128)S(1)} fusion(f32[32,2,64,16]{3,2,1,0:T(8,128)} %reshape_reshape.6, s32[16]{0:T(128)S(1)} %iota_add_fusion.1, s32[32]{0:T(128)S(1)} %fusion.84), kind=kOutput, calls=%fused_computation.61 | convolution fusion | flops 12590080 | bytes 1310912 | tf_op jit(solution)/shard_map/qr,kcr->qkc/dot_general | solution.py:44
  91.0 2.0 reshape_reshape.7
  93.1 4.5 %fusion.43 = f32[32,32,64]{2,0,1:T(8,128)S(1)} fusion(f32[32,2,64,16]{3,2,1,0:T(8,128)} %reshape_reshape.7, s32[16]{0:T(128)S(1)} %iota_add_fusion.1, s32[32]{0:T(128)S(1)} %fusion.84), kind=kOutput, calls=%fused_computation.64 | convolution fusion | flops 12590080 | bytes 1310912 | tf_op jit(solution)/shard_map/qr,kcr->qkc/dot_general | solution.py:47
  97.6 4.3 %fusion.42 = f32[32,32,64]{2,0,1:T(8,128)S(1)} fusion(f32[32,2,64,16]{3,2,1,0:T(8,128)} %reshape_reshape.7, s32[16]{0:T(128)S(1)} %iota_add_fusion.1, s32[32]{0:T(128)S(1)} %fusion.84), kind=kOutput, calls=%fused_computation.63 | convolution fusion | flops 12590080 | bytes 1310912 | tf_op jit(solution)/shard_map/qr,kcr->qkc/dot_general | solution.py:44
  101.9 4.4 %fusion.23 = f32[32,1,32,64]{3,0,2,1:T(8,128)S(1)} fusion(f32[32,32,64]{2,0,1:T(8,128)S(1)} %fusion.41, f32[32,2,64,16]{3,2,1,0:T(8,128)} %reshape_reshape.6, s32[16]{0:T(128)S(1)} %iota_add_fusion.1, s32[32]{0:T(128)S(1)} %fusion.84), kind=kOutput, calls=%fused_computation.40 | convolution fusion | flops 12655616 | bytes 1573056 | tf_op jit(solution)/shard_map/qr,kcr->qkc/dot_general | solution.py:47
  106.3 3.2 %fusion.24 = f32[32,1,32,64]{3,0,2,1:T(8,128)S(1)} fusion(f32[32,32,64]{2,0,1:T(8,128)S(1)} %fusion.40, f32[32,2,64,16]{3,2,1,0:T(8,128)S(1)} %copy-done.2, s32[16]{0:T(128)S(1)} %iota_add_fusion.1, s32[32]{0:T(128)S(1)} %fusion.84), kind=kOutput, calls=%fused_computation.42 | convolution fusion | flops 12655616 | bytes 1836032 | tf_op jit(solution)/shard_map/qr,kcr->qkc/dot_general | solution.py:44
  109.5 3.3 %fusion.21 = f32[32,1,32,64]{3,0,2,1:T(8,128)S(1)} fusion(f32[32,32,64]{2,0,1:T(8,128)S(1)} %fusion.43, f32[32,2,64,16]{3,2,1,0:T(8,128)S(1)} %copy-done.3, s32[16]{0:T(128)S(1)} %iota_add_fusion.1, s32[32]{0:T(128)S(1)} %fusion.84), kind=kOutput, calls=%fused_computation.36 | convolution fusion | flops 12655616 | bytes 1836032 | tf_op jit(solution)/shard_map/qr,kcr->qkc/dot_general | solution.py:47
  112.8 3.1 %fusion.22 = f32[32,1,32,64]{3,0,2,1:T(8,128)S(1)} fusion(f32[32,32,64]{2,0,1:T(8,128)S(1)} %fusion.42, f32[32,2,64,16]{3,2,1,0:T(8,128)S(1)} %copy-done.3, s32[16]{0:T(128)S(1)} %iota_add_fusion.1, s32[32]{0:T(128)S(1)} %fusion.84), kind=kOutput, calls=%fused_computation.38 | convolution fusion | flops 12655616 | bytes 1836032 | tf_op jit(solution)/shard_map/qr,kcr->qkc/dot_general | solution.py:44
  115.9 1.6 pad_maximum_fusion.2
  117.6 44.0 %reduce-scatter.5.cloned.1.call-done = f32[8,4,32,64]{3,0,2,1:T(8,128)} async-done(((f32[32,4,32,64]{3,0,2,1:T(8,128)}), f32[8,4,32,64]{3,0,2,1:T(8,128)}) %reduce-scatter.5.cloned.1.call-update) | async-done | bytes 262160 | tf_op jit(solution)/shard_map/reduce_scatter | solution.py:87
  162.8 8.6 %fusion.10 = f32[8,32,1,64]{3,2,1,0:T(1,128)S(1)} fusion(bf16[8,32,64,128]{3,2,1,0:T(8,128)(2,1)} %param.9, f32[8,32,64,1]{2,0,1,3:T(8,128)S(1)} %bitcast.134), kind=kOutput, calls=%fused_computation.19 | convolution fusion | flops 12582912 | bytes 4325376 | tf_op jit(solution)/shard_map/qkio,qko->qki/dot_general | solution.py:106
  171.4 6.6 %fusion.16 = f32[8,32,1,64]{3,2,1,0:T(1,128)S(1)} fusion(bf16[8,32,64,128]{3,2,1,0:T(8,128)(2,1)S(1)} %copy-done.11, f32[8,32,64,1]{2,0,1,3:T(8,128)S(1)} %bitcast.135), kind=kOutput, calls=%fused_computation.25 | convolution fusion | flops 12582912 | bytes 4325376 | tf_op jit(solution)/shard_map/qkio,qko->qki/dot_general | solution.py:103
  178.0 6.6 %fusion.14 = f32[8,32,1,64]{3,2,1,0:T(1,128)S(1)} fusion(bf16[8,32,64,128]{3,2,1,0:T(8,128)(2,1)S(1)} %copy-done.11, f32[8,32,64,1]{2,0,1,3:T(8,128)S(1)} %bitcast.136), kind=kOutput, calls=%fused_computation.23 | convolution fusion | flops 12582912 | bytes 4325376 | tf_op jit(solution)/shard_map/qkio,qko->qki/dot_general | solution.py:106
  184.6 6.7 %fusion.12 = f32[8,32,1,64]{3,2,1,0:T(1,128)S(1)} fusion(bf16[8,32,64,128]{3,2,1,0:T(8,128)(2,1)S(1)} %copy-done.11, f32[8,32,64,1]{2,0,1,3:T(8,128)S(1)} %bitcast.137), kind=kOutput, calls=%fused_computation.21 | convolution fusion | flops 12582912 | bytes 4325376 | tf_op jit(solution)/shard_map/qkio,qko->qki/dot_general | solution.py:103
  191.6 21.4 %all_gather.6 = f32[32,2,32,64]{3,0,2,1:T(8,128)S(1)} all-gather(f32[8,2,32,64]{3,0,2,1:T(8,128)S(1)} %pad_maximum_fusion.3), channel_id=1, replica_groups=mesh['parts'=1,'axial'=8,'radial'=4] {'radial'}, dimensions={0}, use_global_device_ids=true | all-gather | bytes 655360 | tf_op jit(solution)/shard_map/all_gather | solution.py:111
  215.6 2.4 convert_element_type.61
  218.1 6.1 %fusion.29 = f32[64,64]{0,1:T(8,128)S(1)} fusion(bf16[64,16,1024]{2,1,0:T(8,128)(2,1)S(1)} %copy-done, bf16[64,16,1024]{2,1,0:T(8,128)(2,1)} %copy-done.4), kind=kOutput, calls=%fused_computation.49 | convolution fusion | flops 134217728 | bytes 4210688 | tf_op jit(solution)/shard_map/dot_general | solution.py:138
  224.1 39.3 %psum.7 = f32[64,64]{0,1:T(8,128)S(1)} all-reduce(f32[64,64]{0,1:T(8,128)S(1)} %fusion.29), channel_id=1, replica_groups=mesh['parts'=1,'axial'=8,'radial'=4] {'axial','radial'}, use_global_device_ids=true, to_apply=%region_2.3 | all-reduce | flops 4096 | bytes 32768 | tf_op jit(solution)/shard_map/psum | solution.py:141
  264.1 4.2 %copy.54 = bf16[8,8,16,1024]{3,1,2,0:T(8,128)(2,1)} copy(bf16[8,8,16,1024]{3,2,1,0:T(8,128)(2,1)} %bitcast.130) | data formatting | bytes 4194304
  268.5 8.5 %multiply_add_fusion = (f32[8,32,64,64]{3,2,1,0:T(8,128)}, f32[8,32,64,64]{3,2,1,0:T(8,128)}) fusion(f32[8,32,64]{2,1,0:T(8,128)S(1)} %copy.40, f32[8,32,64]{2,1,0:T(8,128)S(1)} %copy.39, f32[8,32,64]{2,1,0:T(8,128)S(1)} %copy.38, f32[8,32,64]{2,1,0:T(8,128)S(1)} %copy.37), kind=kLoop, calls=%fused_computation.5 | loop fusion | flops 6291456 | bytes 8650752 | tf_op jit(solution)/shard_map/add | solution.py:95
  277.0 12.2 %pad_maximum_fusion = f32[8,32,64,128]{3,2,1,0:T(8,128)} fusion(f32[8,32,64,64]{3,2,1,0:T(8,128)} %get-tuple-element.15, f32[8,32,64,64]{3,2,1,0:T(8,128)} %get-tuple-element.14), kind=kLoop, calls=%fused_computation.3 | loop fusion | flops 2097152 | bytes 16777216 | tf_op jit(solution)/shard_map/concatenate | solution.py:100
  289.2 4.5 %fusion.137 = f32[1024,1024]{1,0:T(8,128)} fusion(bf16[512,1024]{1,0:T(8,128)(2,1)} %all-gather.2.cloned.1.call-done, bf16[1024,512]{0,1:T(8,128)(2,1)S(1)} %copy-done.6), kind=kOutput, calls=%fused_computation.166 | convolution fusion | flops 1073741824 | bytes 6291456 | tf_op jit(solution)/shard_map/jm,aj->ma/dot_general | solution.py:124
  293.7 5.0 %reshape.173 = f32[64,16384]{1,0:T(8,128)} reshape(f32[1024,1024]{1,0:T(8,128)} %fusion.137) | data formatting | bytes 8388608 | tf_op jit(solution)/shard_map/reshape | solution.py:134
  298.7 3.7 %fusion.1 = bf16[64,16384]{1,0:T(8,128)(2,1)S(1)} fusion(f32[64,16384]{1,0:T(8,128)} %reshape.173, bf16[64,64]{1,0:T(8,128)(2,1)S(1)} %copy-done.10, bf16[64,16384]{1,0:T(8,128)(2,1)} %bitcast.131), kind=kOutput, calls=%fused_computation.2 | convolution fusion | flops 136314880 | bytes 8396800 | tf_op jit(solution)/shard_map/dot_general | solution.py:132
  302.3 2.5 copy.55
  (56 shorter events, 10.9 us)
Async XLA Ops:
  7.2 14.1 %copy-start = (bf16[64,16,1024]{2,1,0:T(8,128)(2,1)S(1)}, bf16[64,16,1024]{2,1,0:T(8,128)(2,1)}, u32[]{:S(2)}) copy-start(bf16[64,16,1024]{2,1,0:T(8,128)(2,1)} %param.5) | copy-start | bytes 6291460
  7.2 72.1 %reduce-scatter.3.cloned.1.call-start = ((), (), s32[]{:S(2)}) async-start(), calls=%async_computation.2 | async-start | bytes 4718592 | tf_op jit(solution)/shard_map/reduce_scatter | solution.py:68
  16.0 5.3 %copy-start.5 = (bf16[1024,512]{0,1:T(8,128)(2,1)}, bf16[1024,512]{0,1:T(8,128)(2,1)S(1)}, u32[]{:S(2)}) copy-start(bf16[1024,512]{0,1:T(8,128)(2,1)S(1)} %convert_element_type.60) | copy-start | bytes 3145732
  19.9 1.3 copy-start.4
  25.1 136.5 %reduce-scatter.5.cloned.1.call-start = ((), (), s32[]{:S(2)}) async-start(), calls=%async_computation.3 | async-start | bytes 2621440 | tf_op jit(solution)/shard_map/reduce_scatter | solution.py:87
  93.1 13.2 %copy-start.2 = (f32[32,2,64,16]{3,2,1,0:T(8,128)S(1)}, f32[32,2,64,16]{3,2,1,0:T(8,128)}, u32[]{:S(2)}) copy-start(f32[32,2,64,16]{3,2,1,0:T(8,128)} %reshape_reshape.6) | copy-start | bytes 786436
  93.1 16.4 %copy-start.3 = (f32[32,2,64,16]{3,2,1,0:T(8,128)S(1)}, f32[32,2,64,16]{3,2,1,0:T(8,128)}, u32[]{:S(2)}) copy-start(f32[32,2,64,16]{3,2,1,0:T(8,128)} %reshape_reshape.7) | copy-start | bytes 786436
  117.5 171.7 %all-gather.2.cloned.1.call-start = ((), (), s32[]{:S(2)}) async-start(), calls=%async_computation.4 | async-start | bytes 1179648 | tf_op jit(solution)/shard_map/all_gather | solution.py:126
  161.5 9.9 %copy-start.11 = (bf16[8,32,64,128]{3,2,1,0:T(8,128)(2,1)S(1)}, bf16[8,32,64,128]{3,2,1,0:T(8,128)(2,1)}, u32[]{:S(2)}) copy-start(bf16[8,32,64,128]{3,2,1,0:T(8,128)(2,1)} %param.9) | copy-start | bytes 12582916
  162.8 21.8 %copy-start.7 = (f32[8,32,64]{2,0,1:T(8,128)}, f32[8,32,64]{2,0,1:T(8,128)S(1)}, u32[]{:S(2)}) copy-start(f32[8,32,64]{2,0,1:T(8,128)S(1)} %get-tuple-element.12) | copy-start | bytes 196612
  218.0 50.3 %copy-start.8 = (f32[8,32,64]{2,0,1:T(8,128)S(1)}, f32[8,32,64]{2,0,1:T(8,128)}, u32[]{:S(2)}) copy-start(f32[8,32,64]{2,0,1:T(8,128)} %copy-done.7) | copy-start | bytes 196612
  218.0 50.4 %copy-start.9 = (f32[8,4,32,64]{3,0,2,1:T(8,128)S(1)}, f32[8,4,32,64]{3,0,2,1:T(8,128)}, u32[]{:S(2)}) copy-start(f32[8,4,32,64]{3,0,2,1:T(8,128)} %reduce-scatter.5.cloned.1.call-done) | copy-start | bytes 786436
  277.0 12.2 %copy-start.6 = (bf16[1024,512]{0,1:T(8,128)(2,1)S(1)}, bf16[1024,512]{0,1:T(8,128)(2,1)}, u32[]{:S(2)}) copy-start(bf16[1024,512]{0,1:T(8,128)(2,1)} %copy-done.5) | copy-start | bytes 3145732
  293.7 5.0 %copy-start.10 = (bf16[64,64]{1,0:T(8,128)(2,1)S(1)}, bf16[64,64]{1,0:T(8,128)(2,1)}, u32[]{:S(2)}) copy-start(bf16[64,64]{1,0:T(8,128)(2,1)} %param.8) | copy-start | bytes 24580
  298.7 6.2 %copy-start.1 = (bf16[64,16,1024]{2,1,0:T(8,128)(2,1)S(1)}, bf16[64,16,1024]{2,1,0:T(8,128)(2,1)}, u32[]{:S(2)}) copy-start(bf16[64,16,1024]{2,1,0:T(8,128)(2,1)} %param.5) | copy-start | bytes 6291460
Sparse Core Ops, SparseCore 0:
  25.2 53.9 reduce-scatter.2
  117.6 43.8 reduce-scatter.4
  218.2 23.7 all-gather.1
where the time goes:
time: 316 us; the launch traced here: 312 us
  waiting for transfers between devices  97.6 us (31%)
  matrix products  78.7 us (25%)
  blocking collectives  60.7 us (19%)
  other arithmetic  35.4 us (11%)
  local copies, waits for them, and re-layouts  24.2 us (8%)
  between operations  14.6 us (5%)
    reduce_scatter x1, waiting for transfers between devices, body(): lax.psum_scatter(jnp.concatenate([part_in.reshape(2 * own_ax * lax.axis_s...  53.6 us
    reduce_scatter x1, waiting for transfers between devices, body(): owned = lax.psum_scatter(stacked, 'radial', scatter_dimension=0, tiled=True)  44 us
    psum x1, blocking collectives, body(): lax.psum(local_weight, ('axial', 'radial'))  39.3 us
    all_gather x1, blocking collectives, body(): piece = lax.all_gather(mode_grad, 'radial', axis=0, tiled=True)  21.4 us
    concatenate x1, other arithmetic, body(): spectral_grad = jnp.concatenate([grad_real, grad_imag], axis=3)  12.2 us
    dot_general x2, matrix products, to_modes(): jnp.einsum('qr,kcr->qkc', cos_r, imag_in, precision=high)  8.82 us
    dot_general x2, matrix products, to_modes(): jnp.einsum('qr,kcr->qkc', cos_r, real_in, precision=high)  8.67 us
    dot_general x1, matrix products, body(): jnp.einsum('qkio,qko->qki', w_imag, dy_real, precision=high)  8.64 us
  transfers between devices with their start and end apart: 3, of which 2 were waited for; matrix products, arithmetic and copies ran while one was open for 10% of the time, Pallas kernels for 0%

commit v1 on v0

--- a/solution.py
+++ b/solution.py
@@ -6,6 +6,18 @@
 
 KA = 256
 KR = 32
+
+
+def collect(shard, axis, dim):
+    ways, here, lap = (lax.axis_size(axis), lax.axis_index(axis), shard.shape[dim])
+    shape = [n * ways if d == dim else n for d, n in enumerate(shard.shape)]
+    full = lax.dynamic_update_slice_in_dim(
+        jnp.zeros(shape, shard.dtype), shard, here * lap, axis=dim
+    )
+    for far in range(1, ways):
+        shard = lax.ppermute(shard, axis, [(d, (d + 1) % ways) for d in range(ways)])
+        full = lax.dynamic_update_slice_in_dim(full, shard, (here - far) % ways * lap, axis=dim)
+    return full
 
 
 def axial_table(first, count, modes, total):
@@ -108,7 +120,7 @@
     )
     mode_grad = jnp.stack([dx_real, dx_imag], axis=1)
     row_first = rad_index * rad_rows
-    piece = lax.all_gather(mode_grad, "radial", axis=0, tiled=True)
+    piece = collect(mode_grad, "radial", 0)
     cos_q, sin_q = radial_table(piece.shape[0], row_first, rad_rows, KR, radial_total)
     piece_real = piece[:, 0]
     piece_imag = piece[:, 1]

time: 316 us -> 322 us (1.019)
  waiting for transfers between devices: 97.6 us -> 123 us
  blocking collectives: 60.7 us -> 38.2 us
    ppermute x0 -> x3, waiting for transfers between devices: none -> 25.8 us  [collect(): lax.ppermute(shard, axis, [(d, (d + 1) % ways) for d in range(ways)])]
    all_gather x1 -> x0, blocking collectives: 21.4 us -> none  [body(): piece = lax.all_gather(mode_grad, 'radial', axis=0, tiled=True)]
  transfers between devices with their start and end apart: 3 -> 6, of which waited for: 2 -> 5; matrix products, arithmetic and copies ran while one was open for 10% -> 10% of each run, Pallas kernels for 0% -> 0%
where the time goes in v1:
time: 322 us; the launch traced here: 317 us
  waiting for transfers between devices  123 us (38%)
  matrix products  78.7 us (24%)
  blocking collectives  38.2 us (12%)
  other arithmetic  35.5 us (11%)
  local copies, waits for them, and re-layouts  25.4 us (8%)
  between operations  14.7 us (5%)
    reduce_scatter x1, waiting for transfers between devices, body(): lax.psum_scatter(jnp.concatenate([part_in.reshape(2 * own_ax * lax.axis_s...  53.6 us
    reduce_scatter x1, waiting for transfers between devices, body(): owned = lax.psum_scatter(stacked, 'radial', scatter_dimension=0, tiled=True)  43.9 us
    psum x1, blocking collectives, body(): lax.psum(local_weight, ('axial', 'radial'))  38.2 us
    ppermute x3, waiting for transfers between devices, collect(): lax.ppermute(shard, axis, [(d, (d + 1) % ways) for d in range(ways)])  25.8 us
    concatenate x1, other arithmetic, body(): spectral_grad = jnp.concatenate([grad_real, grad_imag], axis=3)  12.2 us
    dot_general x2, matrix products, to_modes(): jnp.einsum('qr,kcr->qkc', cos_r, imag_in, precision=high)  8.82 us
    dot_general x2, matrix products, to_modes(): jnp.einsum('qr,kcr->qkc', cos_r, real_in, precision=high)  8.67 us
    dot_general x1, matrix products, body(): jnp.einsum('qkio,qko->qki', w_imag, dy_real, precision=high)  8.64 us
  transfers between devices with their start and end apart: 6, of which 5 were waited for; matrix products, arithmetic and copies ran while one was open for 10% of the time, Pallas kernels for 0%

profile of v1, /device:TPU:0, one launch (start us, length us, event | category | flops | bytes accessed | tf_op | source)
XLA Modules:
  0.0 316.7 jit_solution(664023375269989769)
XLA Ops:
  7.2 5.0 %fusion.44 = (bf16[1024,256,1]{1,0,2:T(8,128)(2,1)S(1)}, bf16[1024,256,1]{1,0,2:T(8,128)(2,1)S(1)}) fusion(s32[1024]{0:T(1024)S(1)} %iota_add_fusion), kind=kLoop, calls=%fused_computation.67 | loop fusion | flops 4456448 | bytes 1052672 | tf_op jit(solution)/shard_map/cos | solution.py:30
  12.4 2.1 copy.31
  16.0 3.9 %fusion.9 = bf16[64,16,1024]{2,1,0:T(8,128)(2,1)S(1)} fusion(bf16[64,16,1024]{2,1,0:T(8,128)(2,1)} %param.6, bf16[64,16,1024]{2,1,0:T(8,128)(2,1)} %param.7), kind=kLoop, calls=%fused_computation.18 | loop fusion | flops 12582912 | bytes 6291456 | tf_op jit(solution)/shard_map/convert_element_type | solution.py:75
  22.5 2.5 pad_maximum_fusion.1
  25.7 53.6 %reduce-scatter.3.cloned.1.call-done = f32[64,2048]{1,0:T(8,128)} async-done(((f32[512,2048]{1,0:T(8,128)}), f32[64,2048]{1,0:T(8,128)}) %reduce-scatter.3.cloned.1.call-update) | async-done | bytes 524304 | tf_op jit(solution)/shard_map/reduce_scatter | solution.py:80
  82.4 4.3 %fusion.41 = f32[32,32,64]{2,0,1:T(8,128)S(1)} fusion(f32[32,2,64,16]{3,2,1,0:T(8,128)} %reshape_reshape.6, s32[16]{0:T(128)S(1)} %iota_add_fusion.1, s32[32]{0:T(128)S(1)} %fusion.96), kind=kOutput, calls=%fused_computation.62 | convolution fusion | flops 12590080 | bytes 1310912 | tf_op jit(solution)/shard_map/qr,kcr->qkc/dot_general | solution.py:59
  86.7 4.3 %fusion.40 = f32[32,32,64]{2,0,1:T(8,128)S(1)} fusion(f32[32,2,64,16]{3,2,1,0:T(8,128)} %reshape_reshape.6, s32[16]{0:T(128)S(1)} %iota_add_fusion.1, s32[32]{0:T(128)S(1)} %fusion.96), kind=kOutput, calls=%fused_computation.61 | convolution fusion | flops 12590080 | bytes 1310912 | tf_op jit(solution)/shard_map/qr,kcr->qkc/dot_general | solution.py:56
  91.1 2.0 reshape_reshape.7
  93.1 4.5 %fusion.43 = f32[32,32,64]{2,0,1:T(8,128)S(1)} fusion(f32[32,2,64,16]{3,2,1,0:T(8,128)} %reshape_reshape.7, s32[16]{0:T(128)S(1)} %iota_add_fusion.1, s32[32]{0:T(128)S(1)} %fusion.96), kind=kOutput, calls=%fused_computation.64 | convolution fusion | flops 12590080 | bytes 1310912 | tf_op jit(solution)/shard_map/qr,kcr->qkc/dot_general | solution.py:59
  97.6 4.3 %fusion.42 = f32[32,32,64]{2,0,1:T(8,128)S(1)} fusion(f32[32,2,64,16]{3,2,1,0:T(8,128)} %reshape_reshape.7, s32[16]{0:T(128)S(1)} %iota_add_fusion.1, s32[32]{0:T(128)S(1)} %fusion.96), kind=kOutput, calls=%fused_computation.63 | convolution fusion | flops 12590080 | bytes 1310912 | tf_op jit(solution)/shard_map/qr,kcr->qkc/dot_general | solution.py:56
  101.9 4.4 %fusion.23 = f32[32,1,32,64]{3,0,2,1:T(8,128)S(1)} fusion(f32[32,32,64]{2,0,1:T(8,128)S(1)} %fusion.41, f32[32,2,64,16]{3,2,1,0:T(8,128)} %reshape_reshape.6, s32[16]{0:T(128)S(1)} %iota_add_fusion.1, s32[32]{0:T(128)S(1)} %fusion.96), kind=kOutput, calls=%fused_computation.40 | convolution fusion | flops 12655616 | bytes 1573056 | tf_op jit(solution)/shard_map/qr,kcr->qkc/dot_general | solution.py:59
  106.3 3.2 fusion.24
  109.5 3.3 %fusion.21 = f32[32,1,32,64]{3,0,2,1:T(8,128)S(1)} fusion(f32[32,32,64]{2,0,1:T(8,128)S(1)} %fusion.43, f32[32,2,64,16]{3,2,1,0:T(8,128)S(1)} %copy-done.3, s32[16]{0:T(128)S(1)} %iota_add_fusion.1, s32[32]{0:T(128)S(1)} %fusion.96), kind=kOutput, calls=%fused_computation.36 | convolution fusion | flops 12655616 | bytes 1836032 | tf_op jit(solution)/shard_map/qr,kcr->qkc/dot_general | solution.py:59
  112.8 3.1 fusion.22
  117.6 43.9 %reduce-scatter.5.cloned.1.call-done = f32[8,4,32,64]{3,0,2,1:T(8,128)} async-done(((f32[32,4,32,64]{3,0,2,1:T(8,128)}), f32[8,4,32,64]{3,0,2,1:T(8,128)}) %reduce-scatter.5.cloned.1.call-update) | async-done | bytes 262160 | tf_op jit(solution)/shard_map/reduce_scatter | solution.py:99
  162.8 8.6 %fusion.10 = f32[8,32,1,64]{3,2,1,0:T(1,128)S(1)} fusion(bf16[8,32,64,128]{3,2,1,0:T(8,128)(2,1)} %param.9, f32[8,32,64,1]{2,0,1,3:T(8,128)S(1)} %bitcast.134), kind=kOutput, calls=%fused_computation.19 | convolution fusion | flops 12582912 | bytes 4325376 | tf_op jit(solution)/shard_map/qkio,qko->qki/dot_general | solution.py:118
  171.4 6.6 %fusion.16 = f32[8,32,1,64]{3,2,1,0:T(1,128)S(1)} fusion(bf16[8,32,64,128]{3,2,1,0:T(8,128)(2,1)S(1)} %copy-done.11, f32[8,32,64,1]{2,0,1,3:T(8,128)S(1)} %bitcast.135), kind=kOutput, calls=%fused_computation.25 | convolution fusion | flops 12582912 | bytes 4325376 | tf_op jit(solution)/shard_map/qkio,qko->qki/dot_general | solution.py:115
  178.0 6.6 %fusion.14 = f32[8,32,1,64]{3,2,1,0:T(1,128)S(1)} fusion(bf16[8,32,64,128]{3,2,1,0:T(8,128)(2,1)S(1)} %copy-done.11, f32[8,32,64,1]{2,0,1,3:T(8,128)S(1)} %bitcast.136), kind=kOutput, calls=%fused_computation.23 | convolution fusion | flops 12582912 | bytes 4325376 | tf_op jit(solution)/shard_map/qkio,qko->qki/dot_general | solution.py:118
  184.6 6.7 %fusion.12 = f32[8,32,1,64]{3,2,1,0:T(1,128)S(1)} fusion(bf16[8,32,64,128]{3,2,1,0:T(8,128)(2,1)S(1)} %copy-done.11, f32[8,32,64,1]{2,0,1,3:T(8,128)S(1)} %bitcast.137), kind=kOutput, calls=%fused_computation.21 | convolution fusion | flops 12582912 | bytes 4325376 | tf_op jit(solution)/shard_map/qkio,qko->qki/dot_general | solution.py:115
  191.8 9.7 %collective-permute-done = f32[8,2,32,64]{3,0,2,1:T(8,128)S(1)} collective-permute-done((f32[8,2,32,64]{3,0,2,1:T(8,128)S(1)}, f32[8,2,32,64]{3,0,2,1:T(8,128)S(1)}, u32[]{:S(2)}, u32[]{:S(2)}) %collective-permute-start) | collective-permute-done | bytes 131104 | tf_op jit(solution)/shard_map/ppermute | solution.py:18
  201.8 8.8 %collective-permute-done.1 = f32[8,2,32,64]{3,0,2,1:T(8,128)} collective-permute-done((f32[8,2,32,64]{3,0,2,1:T(8,128)S(1)}, f32[8,2,32,64]{3,0,2,1:T(8,128)}, u32[]{:S(2)}, u32[]{:S(2)}) %collective-permute-start.1) | collective-permute-done | bytes 131104 | tf_op jit(solution)/shard_map/ppermute | solution.py:18
  211.7 7.3 %collective-permute-done.2 = f32[8,2,32,64]{3,0,2,1:T(8,128)S(1)} collective-permute-done((f32[8,2,32,64]{3,0,2,1:T(8,128)}, f32[8,2,32,64]{3,0,2,1:T(8,128)S(1)}, u32[]{:S(2)}, u32[]{:S(2)}) %collective-permute-start.2) | collective-permute-done | bytes 131104 | tf_op jit(solution)/shard_map/ppermute | solution.py:18
  221.6 2.4 convert_element_type.61
  224.1 6.1 %fusion.29 = f32[64,64]{0,1:T(8,128)S(1)} fusion(bf16[64,16,1024]{2,1,0:T(8,128)(2,1)S(1)} %copy-done, bf16[64,16,1024]{2,1,0:T(8,128)(2,1)} %copy-done.4), kind=kOutput, calls=%fused_computation.49 | convolution fusion | flops 134217728 | bytes 4210688 | tf_op jit(solution)/shard_map/dot_general | solution.py:150
  230.1 38.2 %psum.7 = f32[64,64]{0,1:T(8,128)S(1)} all-reduce(f32[64,64]{0,1:T(8,128)S(1)} %fusion.29), channel_id=1, replica_groups=mesh['parts'=1,'axial'=8,'radial'=4] {'axial','radial'}, use_global_device_ids=true, to_apply=%region_2.3 | all-reduce | flops 4096 | bytes 32768 | tf_op jit(solution)/shard_map/psum | solution.py:153
  269.0 4.2 %copy.54 = bf16[8,8,16,1024]{3,1,2,0:T(8,128)(2,1)} copy(bf16[8,8,16,1024]{3,2,1,0:T(8,128)(2,1)} %bitcast.130) | data formatting | bytes 4194304
  273.4 8.5 %multiply_add_fusion = (f32[8,32,64,64]{3,2,1,0:T(8,128)}, f32[8,32,64,64]{3,2,1,0:T(8,128)}) fusion(f32[8,32,64]{2,1,0:T(8,128)S(1)} %copy.40, f32[8,32,64]{2,1,0:T(8,128)S(1)} %copy.39, f32[8,32,64]{2,1,0:T(8,128)S(1)} %copy.38, f32[8,32,64]{2,1,0:T(8,128)S(1)} %copy.37), kind=kLoop, calls=%fused_computation.5 | loop fusion | flops 6291456 | bytes 8650752 | tf_op jit(solution)/shard_map/add | solution.py:107
  281.9 12.2 %pad_maximum_fusion = f32[8,32,64,128]{3,2,1,0:T(8,128)} fusion(f32[8,32,64,64]{3,2,1,0:T(8,128)} %get-tuple-element.15, f32[8,32,64,64]{3,2,1,0:T(8,128)} %get-tuple-element.14), kind=kLoop, calls=%fused_computation.3 | loop fusion | flops 2097152 | bytes 16777216 | tf_op jit(solution)/shard_map/concatenate | solution.py:112
  294.1 4.5 %fusion.137 = f32[1024,1024]{1,0:T(8,128)} fusion(bf16[512,1024]{1,0:T(8,128)(2,1)} %all-gather.2.cloned.1.call-done, bf16[1024,512]{0,1:T(8,128)(2,1)S(1)} %copy-done.6), kind=kOutput, calls=%fused_computation.170 | convolution fusion | flops 1073741824 | bytes 6291456 | tf_op jit(solution)/shard_map/jm,aj->ma/dot_general | solution.py:136
  298.5 5.0 %reshape.173 = f32[64,16384]{1,0:T(8,128)} reshape(f32[1024,1024]{1,0:T(8,128)} %fusion.137) | data formatting | bytes 8388608 | tf_op jit(solution)/shard_map/reshape | solution.py:146
  303.6 3.7 %fusion.1 = bf16[64,16384]{1,0:T(8,128)(2,1)S(1)} fusion(f32[64,16384]{1,0:T(8,128)} %reshape.173, bf16[64,64]{1,0:T(8,128)(2,1)S(1)} %copy-done.10, bf16[64,16384]{1,0:T(8,128)(2,1)} %bitcast.131), kind=kOutput, calls=%fused_computation.2 | convolution fusion | flops 136314880 | bytes 8396800 | tf_op jit(solution)/shard_map/dot_general | solution.py:144
  307.2 2.5 copy.55
  (65 shorter events, 15.9 us)
Async XLA Ops:
  7.2 14.1 %copy-start = (bf16[64,16,1024]{2,1,0:T(8,128)(2,1)S(1)}, bf16[64,16,1024]{2,1,0:T(8,128)(2,1)}, u32[]{:S(2)}) copy-start(bf16[64,16,1024]{2,1,0:T(8,128)(2,1)} %param.5) | copy-start | bytes 6291460
  7.2 72.1 %reduce-scatter.3.cloned.1.call-start = ((), (), s32[]{:S(2)}) async-start(), calls=%async_computation.2 | async-start | bytes 4718592 | tf_op jit(solution)/shard_map/reduce_scatter | solution.py:80
  16.0 5.3 %copy-start.5 = (bf16[1024,512]{0,1:T(8,128)(2,1)}, bf16[1024,512]{0,1:T(8,128)(2,1)S(1)}, u32[]{:S(2)}) copy-start(bf16[1024,512]{0,1:T(8,128)(2,1)S(1)} %convert_element_type.60) | copy-start | bytes 3145732
  19.9 1.3 copy-start.4
  25.1 136.5 %reduce-scatter.5.cloned.1.call-start = ((), (), s32[]{:S(2)}) async-start(), calls=%async_computation.3 | async-start | bytes 2621440 | tf_op jit(solution)/shard_map/reduce_scatter | solution.py:99
  93.1 13.2 %copy-start.2 = (f32[32,2,64,16]{3,2,1,0:T(8,128)S(1)}, f32[32,2,64,16]{3,2,1,0:T(8,128)}, u32[]{:S(2)}) copy-start(f32[32,2,64,16]{3,2,1,0:T(8,128)} %reshape_reshape.6) | copy-start | bytes 786436
  93.1 16.4 %copy-start.3 = (f32[32,2,64,16]{3,2,1,0:T(8,128)S(1)}, f32[32,2,64,16]{3,2,1,0:T(8,128)}, u32[]{:S(2)}) copy-start(f32[32,2,64,16]{3,2,1,0:T(8,128)} %reshape_reshape.7) | copy-start | bytes 786436
  117.5 176.6 %all-gather.2.cloned.1.call-start = ((), (), s32[]{:S(2)}) async-start(), calls=%async_computation.4 | async-start | bytes 1179648 | tf_op jit(solution)/shard_map/all_gather | solution.py:138
  161.5 9.9 %copy-start.11 = (bf16[8,32,64,128]{3,2,1,0:T(8,128)(2,1)S(1)}, bf16[8,32,64,128]{3,2,1,0:T(8,128)(2,1)}, u32[]{:S(2)}) copy-start(bf16[8,32,64,128]{3,2,1,0:T(8,128)(2,1)} %param.9) | copy-start | bytes 12582916
  162.8 21.8 %copy-start.7 = (f32[8,32,64]{2,0,1:T(8,128)}, f32[8,32,64]{2,0,1:T(8,128)S(1)}, u32[]{:S(2)}) copy-start(f32[8,32,64]{2,0,1:T(8,128)S(1)} %get-tuple-element.12) | copy-start | bytes 196612
  191.8 9.7 %collective-permute-start = (f32[8,2,32,64]{3,0,2,1:T(8,128)S(1)}, f32[8,2,32,64]{3,0,2,1:T(8,128)S(1)}, u32[]{:S(2)}, u32[]{:S(2)}) collective-permute-start(f32[8,2,32,64]{3,0,2,1:T(8,128)S(1)} %get-tuple-element.20), channel_id=1, source_target_pairs={{0,1},{1,2},{2,3},{3,0},{4,5},{5,6},{6,7},{7,4},{8,9},{9,10},{10,1... | collective-permute-start | bytes 393224 | tf_op jit(solution)/shard_map/ppermute | solution.py:18
  201.5 9.1 %collective-permute-start.1 = (f32[8,2,32,64]{3,0,2,1:T(8,128)S(1)}, f32[8,2,32,64]{3,0,2,1:T(8,128)}, u32[]{:S(2)}, u32[]{:S(2)}) collective-permute-start(f32[8,2,32,64]{3,0,2,1:T(8,128)S(1)} %collective-permute-done), channel_id=1, source_target_pairs={{0,1},{1,2},{2,3},{3,0},{4,5},{5,6},{6,7},{7,4},{8,9},{9,10},{10,1... | collective-permute-start | bytes 393224 | tf_op jit(solution)/shard_map/ppermute | solution.py:18
  210.6 8.4 %collective-permute-start.2 = (f32[8,2,32,64]{3,0,2,1:T(8,128)}, f32[8,2,32,64]{3,0,2,1:T(8,128)S(1)}, u32[]{:S(2)}, u32[]{:S(2)}) collective-permute-start(f32[8,2,32,64]{3,0,2,1:T(8,128)} %collective-permute-done.1), channel_id=1, source_target_pairs={{0,1},{1,2},{2,3},{3,0},{4,5},{5,6},{6,7},{7,4},{8,9},{9,10},{10,1... | collective-permute-start | bytes 393224 | tf_op jit(solution)/shard_map/ppermute | solution.py:18
  224.0 49.2 %copy-start.8 = (f32[8,32,64]{2,0,1:T(8,128)S(1)}, f32[8,32,64]{2,0,1:T(8,128)}, u32[]{:S(2)}) copy-start(f32[8,32,64]{2,0,1:T(8,128)} %copy-done.7) | copy-start | bytes 196612
  224.0 49.3 %copy-start.9 = (f32[8,4,32,64]{3,0,2,1:T(8,128)S(1)}, f32[8,4,32,64]{3,0,2,1:T(8,128)}, u32[]{:S(2)}) copy-start(f32[8,4,32,64]{3,0,2,1:T(8,128)} %reduce-scatter.5.cloned.1.call-done) | copy-start | bytes 786436
  281.9 12.2 %copy-start.6 = (bf16[1024,512]{0,1:T(8,128)(2,1)S(1)}, bf16[1024,512]{0,1:T(8,128)(2,1)}, u32[]{:S(2)}) copy-start(bf16[1024,512]{0,1:T(8,128)(2,1)} %copy-done.5) | copy-start | bytes 3145732
  298.5 5.0 %copy-start.10 = (bf16[64,64]{1,0:T(8,128)(2,1)S(1)}, bf16[64,64]{1,0:T(8,128)(2,1)}, u32[]{:S(2)}) copy-start(bf16[64,64]{1,0:T(8,128)(2,1)} %param.8) | copy-start | bytes 24580
  303.6 6.2 %copy-start.1 = (bf16[64,16,1024]{2,1,0:T(8,128)(2,1)S(1)}, bf16[64,16,1024]{2,1,0:T(8,128)(2,1)}, u32[]{:S(2)}) copy-start(bf16[64,16,1024]{2,1,0:T(8,128)(2,1)} %param.5) | copy-start | bytes 6291460
Sparse Core Ops, SparseCore 0:
  25.2 54.0 reduce-scatter.2
  117.7 43.8 reduce-scatter.4
  224.2 21.8 all-gather.1
